TPU v7x, 32 devices: a whole 2x2x4 slice. The times are simulated.
32 devices in a mesh: gz: 2 (over y), xy: 16 (over z, x, core).
Axes of the slice: x: 2, y: 2, z: 4, core: 2. Of those that a mesh axis runs over, the one named last changes fastest.
Arguments:
- stack: bfloat16 [32, 256, 2048], P('gz', 'xy'), may hold values from -8 to 8
Outputs:
- joined: float32 [256, 2048], P('xy', 'gz')
- pooled: float32 [128, 1024], P('xy', 'gz')
All inputs are finite; a program needn't handle non-finite values.
Results may differ from a plain program's by a relative error of at most 0.0003.
Values may be sent and summed in bfloat16 or wider, within the bound.
A program may use at most 128 MiB of HBM per device.

v0:
```python
import jax
import jax.numpy as jnp
from jax import lax
from jax.sharding import PartitionSpec as P

sharpness = 0.016
laplace_taps = (
    (0, 0, 16.0),
    (1, 0, -2.0),
    (-1, 0, -2.0),
    (0, 1, -2.0),
    (0, -1, -2.0),
    (1, 1, -1.0),
    (1, -1, -1.0),
    (-1, 1, -1.0),
    (-1, -1, -1.0),
    (2, 0, -1.0),
    (-2, 0, -1.0),
    (0, 2, -1.0),
    (0, -2, -1.0),
)


def with_halo(cells, sides, width):
    for axis, dim in sides:
        count = lax.axis_size(axis)
        ends = count - 1
        head = lax.slice_in_dim(cells, 0, width, axis=dim)
        tail = lax.slice_in_dim(cells, cells.shape[dim] - width, cells.shape[dim], axis=dim)
        cells = jnp.concatenate(
            [
                lax.ppermute(tail, axis, [(i, (i + 1) % count) for i in range(ends)]),
                cells,
                lax.ppermute(head, axis, [((i + 1) % count, i) for i in range(ends)]),
            ],
            axis=dim,
        )
    return cells


def merged(value, axis, join):
    pieces = jax.tree.map(lambda part: lax.all_gather(part, axis), value)
    head = jax.tree.map(lambda part: part[0], pieces)
    tail = jax.tree.map(lambda part: part[1:], pieces)
    running, _ = lax.scan(lambda running, slab: (join(running, slab), None), head, tail)
    return running


def column_shift(values, col_step):
    if col_step == 0:
        return values
    breadth = values.shape[-1]
    if col_step > 0:
        return jnp.pad(values[..., col_step:], ((0, 0), (0, 0), (0, col_step)))
    return jnp.pad(values[..., : breadth + col_step], ((0, 0), (0, 0), (-col_step, 0)))


def laplace_rows(padded, out_rows):
    total = None
    for row_step, col_step, weight in laplace_taps:
        rows_view = padded[:, 2 + row_step : 2 + row_step + out_rows, :].astype(jnp.float32)
        term = weight * column_shift(rows_view, col_step)
        total = term if total is None else total + term
    return total


def box_rows(padded, out_rows):
    row_total = padded[:, 0:out_rows, :]
    for shift_amount in range(-1, 3):
        row_total = row_total + padded[:, 2 + shift_amount : 2 + shift_amount + out_rows, :]
    box_total = column_shift(row_total, -2)
    for shift_amount in range(-1, 3):
        box_total = box_total + column_shift(row_total, shift_amount)
    return box_total


def blend_pair(first, second):
    joint_max = jnp.maximum(first[0], second[0])
    first_scale = jnp.exp(first[0] - joint_max)
    second_scale = jnp.exp(second[0] - joint_max)
    return (
        joint_max,
        first[1] * first_scale + second[1] * second_scale,
        first[2] * first_scale + second[2] * second_scale,
    )


def shards(stack):
    row_count = stack.shape[1]
    col_count = stack.shape[2]
    rimmed = with_halo(stack, (("xy", 1),), 2)
    laplace_out = laplace_rows(rimmed, row_count)
    energy = laplace_out * laplace_out
    energy_wide = with_halo(energy, (("xy", 1),), 2)
    score = box_rows(energy_wide, row_count) * sharpness
    local_max = jnp.max(score, axis=0)
    weights = jnp.exp(score - local_max[None, :, :])
    weighted_sum = jnp.sum(weights * stack.astype(jnp.float32), axis=0)
    weight_sum = jnp.sum(weights, axis=0)
    own_cols = col_count // lax.axis_size("gz")
    joint_max, merged_weighted, merged_weights = merged(
        (local_max, weighted_sum, weight_sum), "gz", blend_pair
    )
    col_start = lax.axis_index("gz") * own_cols
    own_weighted = lax.dynamic_slice_in_dim(merged_weighted, col_start, own_cols, 1)
    own_weights = lax.dynamic_slice_in_dim(merged_weights, col_start, own_cols, 1)
    joined = own_weighted / own_weights
    pooled = joined.reshape(row_count // 2, 2, own_cols // 2, 2).mean(axis=(1, 3))
    return (joined, pooled)


def solution(mesh):
    in_specs = (P("gz", "xy", None),)
    out_specs = (P("xy", "gz"), P("xy", "gz"))
    return jax.shard_map(shards, mesh=mesh, in_specs=in_specs, out_specs=out_specs, check_vma=False)
```

profile of v0, /device:TPU:12, one launch (start us, length us, event | category | flops | bytes accessed | tf_op | source)
XLA Modules:
  0.0 66.5 jit_solution(13230952683840854176)
XLA Ops:
  0.6 1.4 %fusion.20 = (bf16[16,2,2048]{2,1,0:T(2,128)(2,1)S(1)}, bf16[16,2,2048]{2,1,0:T(2,128)(2,1)S(1)}) fusion(bf16[16,16,2048]{2,1,0:T(8,128)(2,1)} %param.1), kind=kLoop, calls=%fused_computation.44 | loop fusion | bytes 524288 | tf_op jit(solution)/shard_map/slice | solution.py:28
  2.1 1.9 %collective-permute-start.1 = (bf16[16,2,2048]{2,0,1:T(8,128)(2,1)S(1)}, bf16[16,2,2048]{2,0,1:T(8,128)(2,1)S(1)}, u32[]{:S(2)}, u32[]{:S(2)}) collective-permute-start(bf16[16,2,2048]{2,0,1:T(8,128)(2,1)S(1)} %copy.13), channel_id=1, source_target_pairs={{0,1},{1,2},{2,3},{3,4},{4,5},{5,6},{6,7},{7,8},{8,9},{9,10},{10,1... | collective-permute-start | bytes 393224 | tf_op jit(solution)/shard_map/ppermute | solution.py:32
  4.1 4.5 %collective-permute-start = (bf16[16,2,2048]{2,0,1:T(8,128)(2,1)S(1)}, bf16[16,2,2048]{2,0,1:T(8,128)(2,1)S(1)}, u32[]{:S(2)}, u32[]{:S(2)}) collective-permute-start(bf16[16,2,2048]{2,0,1:T(8,128)(2,1)S(1)} %copy.14), channel_id=1, source_target_pairs={{1,0},{2,1},{3,2},{4,3},{5,4},{6,5},{7,6},{8,7},{9,8},{10,9},{11,1... | collective-permute-start | bytes 393224 | tf_op jit(solution)/shard_map/ppermute | solution.py:34
  8.6 0.7 collective-permute-done.1
  9.3 1.9 %constant_dynamic-update-slice_fusion.1 = (bf16[16,18,2048]{2,0,1:T(8,128)(2,1)S(1)}, f32[16,16,2048]{2,0,1:T(8,128)S(1)}, bf16[16,18,2048]{2,0,1:T(8,128)(2,1)S(1)}) fusion(bf16[16,16,2048]{2,1,0:T(8,128)(2,1)} %param.1, bf16[16,18,2048]{2,0,1:T(8,128)(2,1)S(1)} %constant_dynamic-update-slice_fusion.3), kind=kLoop, calls=%fused_computation.31 | loop fusion | flops 524287 | bytes 5242880
  11.2 0.2 slice_convert_fusion
  11.5 1.7 %fusion.16 = (f32[16,16,2047]{2,0,1:T(8,128)S(1)}, f32[16,16,2047]{2,0,1:T(8,128)S(1)}, f32[16,16,2047]{2,0,1:T(8,128)S(1)}, f32[16,16,2047]{2,0,1:T(8,128)S(1)}) fusion(f32[16,16,2048]{2,0,1:T(8,128)S(1)} %get-tuple-element.44, f32[16,16,2048]{2,0,1:T(8,128)S(1)} %slice_convert_fusion), kind=kLoop, calls=%fused_computation.40 | loop fusion | bytes 16769024 | tf_op jit(solution)/shard_map/slice | solution.py:54
  13.2 0.8 %fusion.19 = (f32[16,16,2046]{2,0,1:T(8,128)S(1)}, f32[16,16,2046]{2,0,1:T(8,128)S(1)}) fusion(f32[16,16,2048]{2,0,1:T(8,128)S(1)} %get-tuple-element.44), kind=kLoop, calls=%fused_computation.43 | loop fusion | bytes 8380416 | tf_op jit(solution)/shard_map/slice | solution.py:54
  14.0 0.0 collective-permute-done
  14.0 0.2 slice_convert_fusion.1
  14.2 0.0 copy-start
  14.3 0.8 %fusion.17 = (f32[16,16,2047]{2,0,1:T(8,128)S(1)}, f32[16,16,2047]{2,0,1:T(8,128)S(1)}) fusion(f32[16,16,2048]{2,0,1:T(8,128)S(1)} %slice_convert_fusion.1), kind=kLoop, calls=%fused_computation.41 | loop fusion | bytes 8384512 | tf_op jit(solution)/shard_map/slice | solution.py:54
  15.1 0.4 copy-done
  15.5 5.5 %add_multiply_fusion.1 = f32[16,16,2048]{2,0,1:T(8,128)S(1)} fusion(f32[16,16,2046]{2,0,1:T(8,128)S(1)} %get-tuple-element.40, f32[16,16,2046]{2,0,1:T(8,128)S(1)} %get-tuple-element.39, f32[16,16,2047]{2,0,1:T(8,128)S(1)} %get-tuple-element.52, f32[16,16,2047]{2,0,1:T(8,128)S(1)} %get-tuple-element.53, f32[16,16,2047]{2,0,1:T(8,128)S(1)} %get-tuple-element.36, ...), kind=kLoop, calls=%fused_computation.15 | loop fusion | flops 16252928 | bytes 24107008 | tf_op jit(solution)/shard_map/mul | solution.py:93
  21.0 0.8 %fusion.15 = (f32[16,2,2048]{2,0,1:T(8,128)}, f32[16,2,2048]{2,0,1:T(8,128)}) fusion(f32[16,16,2048]{2,0,1:T(8,128)S(1)} %add_multiply_fusion.1), kind=kLoop, calls=%fused_computation.39 | loop fusion | bytes 1048576 | tf_op jit(solution)/shard_map/slice | solution.py:29
  21.8 1.9 %collective-permute-start.2 = (f32[16,2,2048]{2,0,1:T(8,128)}, f32[16,2,2048]{2,0,1:T(8,128)S(1)}, u32[]{:S(2)}, u32[]{:S(2)}) collective-permute-start(f32[16,2,2048]{2,0,1:T(8,128)} %get-tuple-element.31), channel_id=1, source_target_pairs={{0,1},{1,2},{2,3},{3,4},{4,5},{5,6},{6,7},{7,8},{8,9},{9,10},{10,1... | collective-permute-start | bytes 786440 | tf_op jit(solution)/shard_map/ppermute | solution.py:32
  23.8 4.5 %collective-permute-start.3 = (f32[16,2,2048]{2,0,1:T(8,128)}, f32[16,2,2048]{2,0,1:T(8,128)}, u32[]{:S(2)}, u32[]{:S(2)}) collective-permute-start(f32[16,2,2048]{2,0,1:T(8,128)} %get-tuple-element.32), channel_id=1, source_target_pairs={{1,0},{2,1},{3,2},{4,3},{5,4},{6,5},{7,6},{8,7},{9,8},{10,9},{11,1... | collective-permute-start | bytes 786440 | tf_op jit(solution)/shard_map/ppermute | solution.py:34
  28.3 2.4 %collective-permute-done.2 = f32[16,2,2048]{2,0,1:T(8,128)S(1)} collective-permute-done((f32[16,2,2048]{2,0,1:T(8,128)}, f32[16,2,2048]{2,0,1:T(8,128)S(1)}, u32[]{:S(2)}, u32[]{:S(2)}) %collective-permute-start.2) | collective-permute-done | bytes 262176 | tf_op jit(solution)/shard_map/ppermute | solution.py:32
  30.7 1.8 %collective-permute-done.3 = f32[16,2,2048]{2,0,1:T(8,128)} collective-permute-done((f32[16,2,2048]{2,0,1:T(8,128)}, f32[16,2,2048]{2,0,1:T(8,128)}, u32[]{:S(2)}, u32[]{:S(2)}) %collective-permute-start.3) | collective-permute-done | bytes 262176 | tf_op jit(solution)/shard_map/ppermute | solution.py:34
  32.5 1.8 %fusion.2 = f32[16,16,2048]{2,0,1:T(8,128)S(1)} fusion(f32[16,16,2048]{2,0,1:T(8,128)S(1)} %add_multiply_fusion.1, f32[16,2,2048]{2,0,1:T(8,128)} %collective-permute-done.3, f32[16,2,2048]{2,0,1:T(8,128)S(1)} %collective-permute-done.2), kind=kLoop, calls=%fused_computation.6 | loop fusion | flops 4194304 | bytes 4718592 | tf_op jit(solution)/shard_map/add | solution.py:70
  34.3 0.8 %fusion.13 = (f32[16,16,2046]{2,0,1:T(8,128)S(1)}, f32[16,16,2046]{2,0,1:T(8,128)S(1)}) fusion(f32[16,16,2048]{2,0,1:T(8,128)S(1)} %fusion.2), kind=kLoop, calls=%fused_computation.37 | loop fusion | bytes 8380416 | tf_op jit(solution)/shard_map/slice | solution.py:55
  35.1 0.8 %fusion.14 = (f32[16,16,2047]{2,0,1:T(8,128)S(1)}, f32[16,16,2047]{2,0,1:T(8,128)S(1)}) fusion(f32[16,16,2048]{2,0,1:T(8,128)S(1)} %fusion.2), kind=kLoop, calls=%fused_computation.38 | loop fusion | bytes 8384512 | tf_op jit(solution)/shard_map/slice | solution.py:55
  35.8 1.5 %fusion.12 = (f32[16,2048]{1,0:T(8,128)S(1)}, f32[16,16,2048]{2,0,1:T(8,128)S(1)}) fusion(f32[16,16,2046]{2,0,1:T(8,128)S(1)} %get-tuple-element.28, f32[16,16,2047]{2,0,1:T(8,128)S(1)} %get-tuple-element.30, f32[16,16,2048]{2,0,1:T(8,128)S(1)} %fusion.2, f32[16,16,2047]{2,0,1:T(8,128)S(1)} %get-tuple-element.29, f32[16,16,2046]{2,0,1:T(8,128)S(1)} %get-tuple-element.20), kind=kLoop, calls=%fused_computation.36 | loop fusion | flops 3112960 | bytes 12707840 | tf_op jit(solution)/shard_map/reduce_max | solution.py:96
  37.4 6.9 %all-gather.1 = f32[32,2048]{1,0:T(8,128)S(1)} all-gather(f32[16,2048]{1,0:T(8,128)S(1)} %get-tuple-element.18), channel_id=3, replica_groups=mesh['gz'=2,'xy'=16] {'gz'}, dimensions={0}, use_global_device_ids=true | all-gather | bytes 393216 | tf_op jit(solution)/shard_map/all_gather | solution.py:42
  44.3 1.4 %multiply_reduce_fusion = (f32[16,2048]{1,0:T(8,128)S(1)}, f32[16,2048]{1,0:T(8,128)S(1)}) fusion(f32[16,16,2048]{2,0,1:T(8,128)S(1)} %get-tuple-element.19, f32[16,2048]{1,0:T(8,128)S(1)} %get-tuple-element.18, bf16[16,16,2048]{2,1,0:T(8,128)(2,1)S(1)} %copy-done), kind=kLoop, calls=%fused_computation.12 | loop fusion | flops 2555904 | bytes 3538944 | tf_op jit(solution)/shard_map/reduce_sum | solution.py:98
  45.7 6.1 %all-gather = f32[32,2048]{1,0:T(8,128)S(1)} all-gather(f32[16,2048]{1,0:T(8,128)S(1)} %get-tuple-element.16), channel_id=2, replica_groups=mesh['gz'=2,'xy'=16] {'gz'}, dimensions={0}, use_global_device_ids=true | all-gather | bytes 393216 | tf_op jit(solution)/shard_map/all_gather | solution.py:42
  51.8 5.6 %all-gather.2 = f32[32,2048]{1,0:T(8,128)S(1)} all-gather(f32[16,2048]{1,0:T(8,128)S(1)} %get-tuple-element.17), channel_id=4, replica_groups=mesh['gz'=2,'xy'=16] {'gz'}, dimensions={0}, use_global_device_ids=true | all-gather | bytes 393216 | tf_op jit(solution)/shard_map/all_gather | solution.py:42
  57.6 0.0 copy-start.1
  57.6 5.5 %reshape.8 = f32[8,2,512,2]{3,2,1,0:T(8,128)} reshape(f32[16,1024]{1,0:T(8,128)S(1)} %fusion.10) | data formatting | bytes 131072 | tf_op jit(solution)/shard_map/reshape | solution.py:108
  63.1 0.0 copy-done.1
  63.1 2.8 %reduce_sum.29 = f32[8,512]{1,0:T(8,128)S(1)} reduce(f32[8,2,512,2]{3,2,1,0:T(8,128)} %reshape.8, f32[]{:T(128)} %constant.9.clone.1), dimensions={1,3}, to_apply=%region_3.4 | reduce | flops 12288 | bytes 81924 | tf_op jit(solution)/shard_map/reduce_sum | solution.py:108
  65.9 0.6 broadcast_multiply_fusion
  (8 shorter events, 0.2 us)
Async XLA Ops:
  2.1 7.2 %collective-permute-start.1 = (bf16[16,2,2048]{2,0,1:T(8,128)(2,1)S(1)}, bf16[16,2,2048]{2,0,1:T(8,128)(2,1)S(1)}, u32[]{:S(2)}, u32[]{:S(2)}) collective-permute-start(bf16[16,2,2048]{2,0,1:T(8,128)(2,1)S(1)} %copy.13), channel_id=1, source_target_pairs={{0,1},{1,2},{2,3},{3,4},{4,5},{5,6},{6,7},{7,8},{8,9},{9,10},{10,1... | collective-permute-start | bytes 393224 | tf_op jit(solution)/shard_map/ppermute | solution.py:32
  4.1 9.9 %collective-permute-start = (bf16[16,2,2048]{2,0,1:T(8,128)(2,1)S(1)}, bf16[16,2,2048]{2,0,1:T(8,128)(2,1)S(1)}, u32[]{:S(2)}, u32[]{:S(2)}) collective-permute-start(bf16[16,2,2048]{2,0,1:T(8,128)(2,1)S(1)} %copy.14), channel_id=1, source_target_pairs={{1,0},{2,1},{3,2},{4,3},{5,4},{6,5},{7,6},{8,7},{9,8},{10,9},{11,1... | collective-permute-start | bytes 393224 | tf_op jit(solution)/shard_map/ppermute | solution.py:34
  14.2 1.2 %copy-start = (bf16[16,16,2048]{2,1,0:T(8,128)(2,1)S(1)}, bf16[16,16,2048]{2,1,0:T(8,128)(2,1)}, u32[]{:S(2)}) copy-start(bf16[16,16,2048]{2,1,0:T(8,128)(2,1)} %param.1) | copy-start | bytes 3145732
  21.8 8.9 %collective-permute-start.2 = (f32[16,2,2048]{2,0,1:T(8,128)}, f32[16,2,2048]{2,0,1:T(8,128)S(1)}, u32[]{:S(2)}, u32[]{:S(2)}) collective-permute-start(f32[16,2,2048]{2,0,1:T(8,128)} %get-tuple-element.31), channel_id=1, source_target_pairs={{0,1},{1,2},{2,3},{3,4},{4,5},{5,6},{6,7},{7,8},{8,9},{9,10},{10,1... | collective-permute-start | bytes 786440 | tf_op jit(solution)/shard_map/ppermute | solution.py:32
  23.8 8.7 %collective-permute-start.3 = (f32[16,2,2048]{2,0,1:T(8,128)}, f32[16,2,2048]{2,0,1:T(8,128)}, u32[]{:S(2)}, u32[]{:S(2)}) collective-permute-start(f32[16,2,2048]{2,0,1:T(8,128)} %get-tuple-element.32), channel_id=1, source_target_pairs={{1,0},{2,1},{3,2},{4,3},{5,4},{6,5},{7,6},{8,7},{9,8},{10,9},{11,1... | collective-permute-start | bytes 786440 | tf_op jit(solution)/shard_map/ppermute | solution.py:34
  57.6 5.5 %copy-start.1 = (f32[16,1024]{1,0:T(8,128)}, f32[16,1024]{1,0:T(8,128)S(1)}, u32[]{:S(2)}) copy-start(f32[16,1024]{1,0:T(8,128)S(1)} %fusion.10) | copy-start | bytes 196612
where the time goes:
time: 66.9 us; the launch traced here: 66.5 us
  blocking collectives  18.7 us (28%)
  other arithmetic  16.1 us (24%)
  local copies, waits for them, and re-layouts  13.1 us (20%)
  starting transfers between devices  12.9 us (19%)
  waiting for transfers between devices  4.84 us (7%)
  between operations  0.84 us (1%)
    all_gather x3, blocking collectives, merged(): pieces = jax.tree.map(lambda part: lax.all_gather(part, axis), value)  18.7 us
    ppermute x2, starting transfers between devices, with_halo(): lax.ppermute(head, axis, [((i + 1) % count, i) for i in range(ends)])  9.08 us
    mul x1, other arithmetic, shards(): energy = laplace_out * laplace_out  5.52 us
    reshape x1, local copies, waits for them, and re-layouts, shards(): joined.reshape(row_count // 2, 2, own_cols // 2, 2).mean(axis=(1, 3))  5.52 us
    ppermute x2, starting transfers between devices, with_halo(): lax.ppermute(tail, axis, [(i, (i + 1) % count) for i in range(ends)])  3.83 us
    slice x3, local copies, waits for them, and re-layouts, column_shift(): return jnp.pad(values[..., col_step:], ((0, 0), (0, 0), (0, col_step)))  3.3 us
    ppermute x2, waiting for transfers between devices, with_halo(): lax.ppermute(tail, axis, [(i, (i + 1) % count) for i in range(ends)])  3.07 us
    reduce_sum x1, other arithmetic, shards(): joined.reshape(row_count // 2, 2, own_cols // 2, 2).mean(axis=(1, 3))  2.8 us
  transfers between devices with their start and end apart: 4, of which 3 were waited for; matrix products, arithmetic and copies ran while one was open for 7% of the time, Pallas kernels for 0%

commit v1 on v0

v1 whole, which is shorter than its diff:
```python
import functools

import jax
import jax.numpy as jnp
from jax import lax
from jax.experimental import pallas as pl
from jax.experimental.pallas import tpu as pltpu
from jax.sharding import PartitionSpec as P

sharpness = 0.016
LANES = 128
HALO = 4
MESH = pl.DeviceIdType.MESH


def cols(tile, count):
    return pl.ds(pl.multiple_of(tile * LANES, LANES), count * LANES)


def from_left(tiles, step, lane):
    rolled = [pltpu.roll(t, step, 1) for t in tiles]
    return [jnp.where(lane < step, rolled[i], rolled[i + 1]) for i in range(len(tiles) - 1)]


def from_right(tiles, step, lane):
    rolled = [pltpu.roll(t, LANES - step, 1) for t in tiles]
    return [
        jnp.where(lane < LANES - step, rolled[i], rolled[i + 1]) for i in range(len(tiles) - 1)
    ]


def kernel(
    geom, x_hbm, joined_ref, pooled_ref,
    xin, top_in, bot_in, top_out, bot_out, xs, es, vs, ss, own, outbox, inbox, jt,
    load_sem, halo_send, halo_recv, gz_send, gz_recv,
):
    planes, rows, tiles, gz_count, xy_count, own_tiles, groups = geom
    gz = lax.axis_index("gz")
    xy = lax.axis_index("xy")
    has_up = xy > 0
    has_down = xy < xy_count - 1

    if gz_count == 2:
        near = own_tiles + 2
        parts = [
            (jnp.where(gz == 0, tiles - near, 0), near),
            (jnp.where(gz == 0, 0, near), tiles - near),
        ]
    else:
        parts = [(0, tiles)]

    def load(part):
        start, size = parts[part]
        return pltpu.make_async_copy(
            x_hbm.at[:, :, cols(start, size)], xin.at[:, :, cols(start + 1, size)], load_sem.at[part]
        )

    for part in range(len(parts)):
        load(part).start()

    barrier = pltpu.get_barrier_semaphore()

    @pl.when(has_up)
    def _():
        pl.semaphore_signal(barrier, inc=1, device_id={"xy": xy - 1}, device_id_type=MESH)

    @pl.when(has_down)
    def _():
        pl.semaphore_signal(barrier, inc=1, device_id={"xy": xy + 1}, device_id_type=MESH)

    for step in range(gz_count - 1):
        peer = lax.rem(gz + 1 + step, gz_count)
        pl.semaphore_signal(barrier, inc=1, device_id={"gz": peer}, device_id_type=MESH)

    def to_up(part):
        start, size = parts[part]
        return pltpu.make_async_remote_copy(
            src_ref=top_out.at[:, :, cols(start, size)],
            dst_ref=bot_in.at[:, :, cols(start + 1, size)],
            send_sem=halo_send.at[0, part], recv_sem=halo_recv.at[0, part],
            device_id={"xy": xy - 1}, device_id_type=MESH,
        )

    def to_down(part):
        start, size = parts[part]
        return pltpu.make_async_remote_copy(
            src_ref=bot_out.at[:, :, cols(start, size)],
            dst_ref=top_in.at[:, :, cols(start + 1, size)],
            send_sem=halo_send.at[1, part], recv_sem=halo_recv.at[1, part],
            device_id={"xy": xy + 1}, device_id_type=MESH,
        )

    for tile in (0, tiles + 1):
        side = pl.ds(tile * LANES, LANES)
        xin[:, :, side] = jnp.zeros((planes, rows, LANES), xin.dtype)
        top_in[:, :, side] = jnp.zeros((planes, HALO, LANES), xin.dtype)
        bot_in[:, :, side] = jnp.zeros((planes, HALO, LANES), xin.dtype)
        vs[:, tile] = jnp.zeros((planes, rows, LANES), jnp.float32)
    xs[:, rows + 12 : rows + 16, :] = jnp.zeros((xs.shape[0], 4, LANES), jnp.float32)

    inner = pl.ds(LANES, tiles * LANES)

    @pl.when(jnp.logical_not(has_up))
    def _():
        top_in[:, :, inner] = jnp.zeros((planes, HALO, tiles * LANES), xin.dtype)

    @pl.when(jnp.logical_not(has_down))
    def _():
        bot_in[:, :, inner] = jnp.zeros((planes, HALO, tiles * LANES), xin.dtype)

    for part, (start, size) in enumerate(parts):
        load(part).wait()

        @pl.loop(0, planes)
        def _(p):
            top_out[p, :, cols(start, size)] = xin[p, 0:HALO, cols(start + 1, size)]
            bot_out[p, :, cols(start, size)] = xin[p, rows - HALO : rows, cols(start + 1, size)]

        if part == 0:
            neighbours = jnp.where(has_up, 1, 0) + jnp.where(has_down, 1, 0) + gz_count - 1
            pl.semaphore_wait(barrier, neighbours)

        @pl.when(has_up)
        def _():
            to_up(part).start()

        @pl.when(has_down)
        def _():
            to_down(part).start()

    tall = rows + 8
    lane_tall = lax.broadcasted_iota(jnp.int32, (tall, LANES), 1)
    lane = lax.broadcasted_iota(jnp.int32, (rows, LANES), 1)
    row_tall = lax.broadcasted_iota(jnp.int32, (tall, LANES), 0)
    first = jnp.where(has_up, 0, 2)
    last = jnp.where(has_down, rows + 4, rows + 2)
    row_mask = jnp.where((row_tall >= first) & (row_tall < last), 1.0, 0.0).astype(jnp.float32)

    def scores(chunk, e_start, e_count):
        @pl.loop(0, planes)
        def _(p):
            for i in range(e_count + 2):
                here = cols(e_start + i, 1)
                xs[i, 8 : 8 + rows, :] = xin[p, :, here].astype(jnp.float32)
                xs[i, 4:8, :] = top_in[p, :, here].astype(jnp.float32)
                xs[i, 8 + rows : 12 + rows, :] = bot_in[p, :, here].astype(jnp.float32)
            mid, smooth = [], []
            for i in range(e_count + 2):
                centre = xs[i, 6 : 6 + tall, :]
                mid.append(centre)
                smooth.append(
                    xs[i, 5 : 5 + tall, :] + xs[i, 7 : 7 + tall, :] + (centre + centre)
                )
            right = from_right(smooth, 1, lane_tall)
            pair = [smooth[i] + right[i] for i in range(e_count + 1)]
            left = from_left(pair, 1, lane_tall)
            left2 = from_left(mid, 2, lane_tall)
            right2 = from_right(mid, 2, lane_tall)
            for i in range(e_count):
                total = pair[i + 1] + left[i]
                total = total + (left2[i] + right2[i + 1])
                total = total + (xs[i + 1, 4 : 4 + tall, :] + xs[i + 1, 8 : 8 + tall, :])
                laplace = 20.0 * mid[i + 1] - total
                es[i, :, :] = laplace * laplace * row_mask
            for i in range(e_count):
                column = es[i, 0:rows, :]
                for k in range(1, 5):
                    column = column + es[i, k : k + rows, :]
                vs[p, e_start + i + 1] = column
            flat = [vs[p, chunk * own_tiles + i] for i in range(own_tiles + 2)]
            right = from_right(flat, 1, lane)
            pair = [flat[i] + right[i] for i in range(own_tiles + 1)]
            left = from_left(pair, 2, lane)
            right2 = from_right(flat, 2, lane)
            for i in range(own_tiles):
                ss[p, i] = (pair[i + 1] + left[i] + right2[i + 1]) * sharpness

    def finish(chunk, tile, dst):
        peak = ss[0, tile]
        for p in range(1, planes):
            peak = jnp.maximum(peak, ss[p, tile])
        here = cols(chunk * own_tiles + tile + 1, 1)
        total, blend = None, None
        for p in range(planes):
            weight = jnp.exp(ss[p, tile] - peak)
            term = weight * xin[p, :, here].astype(jnp.float32)
            total = weight if total is None else total + weight
            blend = term if blend is None else blend + term
        dst[0] = peak + jnp.log(total)
        dst[1] = blend / total

    group_tiles = own_tiles // groups

    def to_peer(step, group):
        part = pl.ds(group * group_tiles, group_tiles)
        return pltpu.make_async_remote_copy(
            src_ref=outbox.at[step, part], dst_ref=inbox.at[step, part],
            send_sem=gz_send.at[step, group], recv_sem=gz_recv.at[step, group],
            device_id={"gz": lax.rem(gz + 1 + step, gz_count)}, device_id_type=MESH,
        )

    def halo_arrived(part):
        @pl.when(has_down)
        def _():
            to_up(part).wait_recv()

        @pl.when(has_up)
        def _():
            to_down(part).wait_recv()

    for step in range(gz_count):
        chunk = lax.rem(gz + 1 + step, gz_count)
        if step < len(parts):
            halo_arrived(step)
        if gz_count == 2:
            if step == 0:
                e_start, e_count = jnp.where(gz == 0, tiles - own_tiles - 1, 0), own_tiles + 1
            else:
                e_start, e_count = jnp.where(gz == 0, 0, own_tiles + 1), own_tiles - 1
        else:
            e_count = own_tiles + 2
            e_start = jnp.clip(chunk * own_tiles - 1, 0, tiles - e_count)
        scores(chunk, e_start, e_count)
        if step < gz_count - 1:
            for group in range(groups):
                @pl.loop(group * group_tiles, (group + 1) * group_tiles)
                def _(tile):
                    finish(chunk, tile, outbox.at[step, tile])

                to_peer(step, group).start()
        else:
            @pl.loop(0, own_tiles)
            def _(tile):
                finish(chunk, tile, own.at[tile])

    for group in range(groups):
        for step in range(gz_count - 1):
            to_peer(step, group).wait()
        for tile in range(group * group_tiles, (group + 1) * group_tiles):
            logs = [own[tile, 0]] + [inbox[s, tile, 0] for s in range(gz_count - 1)]
            means = [own[tile, 1]] + [inbox[s, tile, 1] for s in range(gz_count - 1)]
            peak = functools.reduce(jnp.maximum, logs)
            shares = [jnp.exp(value - peak) for value in logs]
            blend = sum(share * mean for share, mean in zip(shares, means))
            joined = blend / sum(shares)
            joined_ref[:, tile * LANES : (tile + 1) * LANES] = joined
            jt[tile] = joined

    half = rows // 2
    source = lax.broadcasted_iota(jnp.int32, (2 * LANES, LANES), 0)
    target = lax.broadcasted_iota(jnp.int32, (2 * LANES, LANES), 1)
    gather = jnp.where(lax.div(source, 2) == target, 0.25, 0.0).astype(jnp.float32)
    for pair_index in range(own_tiles // 2):
        sides = []
        for tile in (2 * pair_index, 2 * pair_index + 1):
            sides.append(
                jt[tile, pl.ds(0, half, stride=2), :] + jt[tile, pl.ds(1, half, stride=2), :]
            )
        wide = jnp.concatenate(sides, axis=1)
        pooled_ref[:, pair_index * LANES : (pair_index + 1) * LANES] = jnp.dot(
            wide, gather, precision=lax.Precision.HIGHEST, preferred_element_type=jnp.float32
        )

    for part in range(len(parts)):
        @pl.when(has_up)
        def _():
            to_up(part).wait_send()

        @pl.when(has_down)
        def _():
            to_down(part).wait_send()


def shards(gz_count, xy_count, stack):
    planes, rows, breadth = stack.shape
    tiles = breadth // LANES
    own_tiles = tiles // gz_count
    groups = 2
    geom = (planes, rows, tiles, gz_count, xy_count, own_tiles, groups)
    f32 = jnp.float32
    padded = breadth + 2 * LANES
    spread = own_tiles + 4
    parts = 2 if gz_count == 2 else 1
    return pl.pallas_call(
        functools.partial(kernel, geom),
        out_shape=(
            jax.ShapeDtypeStruct((rows, own_tiles * LANES), f32),
            jax.ShapeDtypeStruct((rows // 2, own_tiles * LANES // 2), f32),
        ),
        in_specs=[pl.BlockSpec(memory_space=pl.ANY)],
        out_specs=(
            pl.BlockSpec(memory_space=pltpu.VMEM),
            pl.BlockSpec(memory_space=pltpu.VMEM),
        ),
        scratch_shapes=[
            pltpu.VMEM((planes, rows, padded), stack.dtype),
            pltpu.VMEM((planes, HALO, padded), stack.dtype),
            pltpu.VMEM((planes, HALO, padded), stack.dtype),
            pltpu.VMEM((planes, HALO, breadth), stack.dtype),
            pltpu.VMEM((planes, HALO, breadth), stack.dtype),
            pltpu.VMEM((spread, rows + 16, LANES), f32),
            pltpu.VMEM((spread, rows + 8, LANES), f32),
            pltpu.VMEM((planes, tiles + 2, rows, LANES), f32),
            pltpu.VMEM((planes, own_tiles, rows, LANES), f32),
            pltpu.VMEM((own_tiles, 2, rows, LANES), f32),
            pltpu.VMEM((gz_count - 1, own_tiles, 2, rows, LANES), f32),
            pltpu.VMEM((gz_count - 1, own_tiles, 2, rows, LANES), f32),
            pltpu.VMEM((own_tiles, rows, LANES), f32),
            pltpu.SemaphoreType.DMA((parts,)),
            pltpu.SemaphoreType.DMA((2, parts)),
            pltpu.SemaphoreType.DMA((2, parts)),
            pltpu.SemaphoreType.DMA((gz_count - 1, groups)),
            pltpu.SemaphoreType.DMA((gz_count - 1, groups)),
        ],
        compiler_params=pltpu.CompilerParams(collective_id=0, has_side_effects=True),
    )(stack)


def solution(mesh):
    body = functools.partial(shards, mesh.shape["gz"], mesh.shape["xy"])
    in_specs = (P("gz", "xy", None),)
    out_specs = (P("xy", "gz"), P("xy", "gz"))
    return jax.shard_map(body, mesh=mesh, in_specs=in_specs, out_specs=out_specs, check_vma=False)
```

time: 66.9 us -> 26.3 us (0.39)
  the two profiles are of different devices: /device:TPU:12 before, /device:TPU:25 now
where the time goes in v1:
time: 26.3 us; the launch traced here: 26.1 us
  Pallas kernels  23.3 us (89%)
  local copies, waits for them, and re-layouts  2.09 us (8%)
  between operations  0.65 us (2%)
    pallas_call x1, Pallas kernels, shards(): pl.pallas_call(functools.partial(kernel, geom), out_shape=(jax.ShapeDtype...  23.3 us
    unnamed x4, local copies, waits for them, and re-layouts  2.09 us

profile of v1, /device:TPU:25, one launch (start us, length us, event | category | flops | bytes accessed | tf_op | source)
XLA Modules:
  0.0 26.1 jit_solution(12692439135875091766)
XLA Ops:
  0.6 23.3 %shard_map.30 = (f32[16,1024]{1,0:T(8,128)}, f32[8,512]{1,0:T(8,128)}) custom-call(bf16[16,16,2048]{2,1,0:T(8,128)(2,1)} %x_hbm.1), custom_call_target="tpu_custom_call" | custom-call | tf_op jit(solution)/shard_map/pallas_call | solution.py:284
  24.0 0.0 copy-start
  24.0 1.5 %copy.5 = f32[16,1024]{1,0:T(8,128)} copy(f32[16,1024]{1,0:T(8,128)} %get-tuple-element.4) | data formatting | bytes 131072
  25.5 0.0 copy-done
  25.5 0.6 %copy.6 = f32[8,512]{1,0:T(8,128)} copy(f32[8,512]{1,0:T(8,128)S(1)} %copy-done) | data formatting | bytes 32768
Async XLA Ops:
  24.0 1.5 %copy-start = (f32[8,512]{1,0:T(8,128)S(1)}, f32[8,512]{1,0:T(8,128)}, u32[]{:S(2)}) copy-start(f32[8,512]{1,0:T(8,128)} %get-tuple-element.5) | copy-start | bytes 49156

commit v2 on v1

--- a/solution.py
+++ b/solution.py
@@ -31,7 +31,7 @@
 
 def kernel(
     geom, x_hbm, joined_ref, pooled_ref,
-    xin, top_in, bot_in, top_out, bot_out, xs, es, vs, ss, own, outbox, inbox, jt,
+    xin, top_in, bot_in, top_out, bot_out, taps, xs, gs, hs, es, vs, ss, own, outbox, inbox, jt,
     load_sem, halo_send, halo_recv, gz_send, gz_recv,
 ):
     planes, rows, tiles, gz_count, xy_count, own_tiles, groups = geom
@@ -75,8 +75,8 @@
     def to_up(part):
         start, size = parts[part]
         return pltpu.make_async_remote_copy(
-            src_ref=top_out.at[:, :, cols(start, size)],
-            dst_ref=bot_in.at[:, :, cols(start + 1, size)],
+            src_ref=top_out.at[:, cols(start, size)],
+            dst_ref=bot_in.at[:, cols(start + 1, size)],
             send_sem=halo_send.at[0, part], recv_sem=halo_recv.at[0, part],
             device_id={"xy": xy - 1}, device_id_type=MESH,
         )
@@ -84,37 +84,54 @@
     def to_down(part):
         start, size = parts[part]
         return pltpu.make_async_remote_copy(
-            src_ref=bot_out.at[:, :, cols(start, size)],
-            dst_ref=top_in.at[:, :, cols(start + 1, size)],
+            src_ref=bot_out.at[:, cols(start, size)],
+            dst_ref=top_in.at[:, cols(start + 1, size)],
             send_sem=halo_send.at[1, part], recv_sem=halo_recv.at[1, part],
             device_id={"xy": xy + 1}, device_id_type=MESH,
         )
 
+    edge = HALO * planes
     for tile in (0, tiles + 1):
         side = pl.ds(tile * LANES, LANES)
         xin[:, :, side] = jnp.zeros((planes, rows, LANES), xin.dtype)
-        top_in[:, :, side] = jnp.zeros((planes, HALO, LANES), xin.dtype)
-        bot_in[:, :, side] = jnp.zeros((planes, HALO, LANES), xin.dtype)
+        top_in[:, side] = jnp.zeros((edge, LANES), xin.dtype)
+        bot_in[:, side] = jnp.zeros((edge, LANES), xin.dtype)
         vs[:, tile] = jnp.zeros((planes, rows, LANES), jnp.float32)
-    xs[:, rows + 12 : rows + 16, :] = jnp.zeros((xs.shape[0], 4, LANES), jnp.float32)
 
     inner = pl.ds(LANES, tiles * LANES)
 
     @pl.when(jnp.logical_not(has_up))
     def _():
-        top_in[:, :, inner] = jnp.zeros((planes, HALO, tiles * LANES), xin.dtype)
+        top_in[:, inner] = jnp.zeros((edge, tiles * LANES), xin.dtype)
 
     @pl.when(jnp.logical_not(has_down))
     def _():
-        bot_in[:, :, inner] = jnp.zeros((planes, HALO, tiles * LANES), xin.dtype)
-
+        bot_in[:, inner] = jnp.zeros((edge, tiles * LANES), xin.dtype)
+
+    low = lax.broadcasted_iota(jnp.int32, (8, LANES), 0) < HALO
     for part, (start, size) in enumerate(parts):
         load(part).wait()
 
-        @pl.loop(0, planes)
-        def _(p):
-            top_out[p, :, cols(start, size)] = xin[p, 0:HALO, cols(start + 1, size)]
-            bot_out[p, :, cols(start, size)] = xin[p, rows - HALO : rows, cols(start + 1, size)]
+        @pl.loop(start, start + size)
+        def _(t):
+            here = cols(t + 1, 1)
+            for p in range(planes):
+                xs[t, p, 8 : 8 + rows, :] = xin[p, :, here].astype(jnp.float32)
+            out = cols(t, 1)
+            for quad in range(planes // 4):
+                tops, bots = [], []
+                for p in (4 * quad, 4 * quad + 2):
+                    tops.append(jnp.where(low, xs[t, p, 8:16, :], xs[t, p + 1, 4:12, :]))
+                    bots.append(
+                        jnp.where(
+                            low,
+                            xs[t, p, 4 + rows : 12 + rows, :],
+                            xs[t, p + 1, rows : 8 + rows, :],
+                        )
+                    )
+                place = slice(16 * quad, 16 * quad + 16)
+                top_out[place, out] = jnp.concatenate(tops, axis=0).astype(xin.dtype)
+                bot_out[place, out] = jnp.concatenate(bots, axis=0).astype(xin.dtype)
 
         if part == 0:
             neighbours = jnp.where(has_up, 1, 0) + jnp.where(has_down, 1, 0) + gz_count - 1
@@ -128,8 +145,23 @@
         def _():
             to_down(part).start()
 
+    source = lax.broadcasted_iota(jnp.int32, (3 * LANES, LANES), 0)
+    target = lax.broadcasted_iota(jnp.int32, (3 * LANES, LANES), 1)
+    apart = jnp.abs(source - target - LANES)
+    centre = jnp.where(apart == 0, 16.0, jnp.where(apart == 1, -2.0, jnp.where(apart == 2, -1.0, 0.0)))
+    beside = jnp.where(apart == 0, -2.0, jnp.where(apart == 1, -1.0, 0.0))
+    taps[:, 0:LANES] = centre.astype(taps.dtype)
+    taps[:, LANES : 2 * LANES] = beside.astype(taps.dtype)
+
+    @pl.loop(0, tiles)
+    def _(t):
+        wide = xin[:, :, cols(t, 3)].reshape(planes * rows, 3 * LANES)
+        both = jnp.dot(wide, taps[...], preferred_element_type=jnp.float32)
+        both = both.reshape(planes, rows, 2 * LANES)
+        hs[t, :, 8 : 8 + rows, :] = both[:, :, 0:LANES]
+        gs[t, :, 8 : 8 + rows, :] = both[:, :, LANES:]
+
     tall = rows + 8
-    lane_tall = lax.broadcasted_iota(jnp.int32, (tall, LANES), 1)
     lane = lax.broadcasted_iota(jnp.int32, (rows, LANES), 1)
     row_tall = lax.broadcasted_iota(jnp.int32, (tall, LANES), 0)
     first = jnp.where(has_up, 0, 2)
@@ -137,30 +169,28 @@
     row_mask = jnp.where((row_tall >= first) & (row_tall < last), 1.0, 0.0).astype(jnp.float32)
 
     def scores(chunk, e_start, e_count):
+        @pl.loop(e_start, e_start + e_count)
+        def _(t):
+            for ref, base in ((top_in, 4), (bot_in, 8 + rows)):
+                both = jnp.dot(
+                    ref[:, cols(t, 3)], taps[...], preferred_element_type=jnp.float32
+                )
+                plain = ref[:, cols(t + 1, 1)].astype(jnp.float32)
+                for p in range(planes):
+                    part = slice(HALO * p, HALO * p + HALO)
+                    hs[t, p, base : base + HALO, :] = both[part, 0:LANES]
+                    gs[t, p, base : base + HALO, :] = both[part, LANES:]
+                    xs[t, p, base : base + HALO, :] = plain[part, :]
+
         @pl.loop(0, planes)
         def _(p):
-            for i in range(e_count + 2):
-                here = cols(e_start + i, 1)
-                xs[i, 8 : 8 + rows, :] = xin[p, :, here].astype(jnp.float32)
-                xs[i, 4:8, :] = top_in[p, :, here].astype(jnp.float32)
-                xs[i, 8 + rows : 12 + rows, :] = bot_in[p, :, here].astype(jnp.float32)
-            mid, smooth = [], []
-            for i in range(e_count + 2):
-                centre = xs[i, 6 : 6 + tall, :]
-                mid.append(centre)
-                smooth.append(
-                    xs[i, 5 : 5 + tall, :] + xs[i, 7 : 7 + tall, :] + (centre + centre)
+            for i in range(e_count):
+                t = e_start + i
+                laplace = (
+                    hs[t, p, 6 : 6 + tall, :]
+                    + (gs[t, p, 5 : 5 + tall, :] + gs[t, p, 7 : 7 + tall, :])
+                    - (xs[t, p, 4 : 4 + tall, :] + xs[t, p, 8 : 8 + tall, :])
                 )
-            right = from_right(smooth, 1, lane_tall)
-            pair = [smooth[i] + right[i] for i in range(e_count + 1)]
-            left = from_left(pair, 1, lane_tall)
-            left2 = from_left(mid, 2, lane_tall)
-            right2 = from_right(mid, 2, lane_tall)
-            for i in range(e_count):
-                total = pair[i + 1] + left[i]
-                total = total + (left2[i] + right2[i + 1])
-                total = total + (xs[i + 1, 4 : 4 + tall, :] + xs[i + 1, 8 : 8 + tall, :])
-                laplace = 20.0 * mid[i + 1] - total
                 es[i, :, :] = laplace * laplace * row_mask
             for i in range(e_count):
                 column = es[i, 0:rows, :]
@@ -179,11 +209,11 @@
         peak = ss[0, tile]
         for p in range(1, planes):
             peak = jnp.maximum(peak, ss[p, tile])
-        here = cols(chunk * own_tiles + tile + 1, 1)
+        place = chunk * own_tiles + tile
         total, blend = None, None
         for p in range(planes):
             weight = jnp.exp(ss[p, tile] - peak)
-            term = weight * xin[p, :, here].astype(jnp.float32)
+            term = weight * xs[place, p, 8 : 8 + rows, :]
             total = weight if total is None else total + weight
             blend = term if blend is None else blend + term
         dst[0] = peak + jnp.log(total)
@@ -287,18 +317,21 @@
             jax.ShapeDtypeStruct((rows, own_tiles * LANES), f32),
             jax.ShapeDtypeStruct((rows // 2, own_tiles * LANES // 2), f32),
         ),
-        in_specs=[pl.BlockSpec(memory_space=pl.ANY)],
+        in_specs=[pl.BlockSpec(memory_space=pltpu.HBM)],
         out_specs=(
             pl.BlockSpec(memory_space=pltpu.VMEM),
             pl.BlockSpec(memory_space=pltpu.VMEM),
         ),
         scratch_shapes=[
             pltpu.VMEM((planes, rows, padded), stack.dtype),
-            pltpu.VMEM((planes, HALO, padded), stack.dtype),
-            pltpu.VMEM((planes, HALO, padded), stack.dtype),
-            pltpu.VMEM((planes, HALO, breadth), stack.dtype),
-            pltpu.VMEM((planes, HALO, breadth), stack.dtype),
-            pltpu.VMEM((spread, rows + 16, LANES), f32),
+            pltpu.VMEM((planes * HALO, padded), stack.dtype),
+            pltpu.VMEM((planes * HALO, padded), stack.dtype),
+            pltpu.VMEM((planes * HALO, breadth), stack.dtype),
+            pltpu.VMEM((planes * HALO, breadth), stack.dtype),
+            pltpu.VMEM((3 * LANES, 2 * LANES), stack.dtype),
+            pltpu.VMEM((tiles, planes, rows + 16, LANES), f32),
+            pltpu.VMEM((tiles, planes, rows + 16, LANES), f32),
+            pltpu.VMEM((tiles, planes, rows + 16, LANES), f32),
             pltpu.VMEM((spread, rows + 8, LANES), f32),
             pltpu.VMEM((planes, tiles + 2, rows, LANES), f32),
             pltpu.VMEM((planes, own_tiles, rows, LANES), f32),
@@ -312,7 +345,7 @@
             pltpu.SemaphoreType.DMA((gz_count - 1, groups)),
             pltpu.SemaphoreType.DMA((gz_count - 1, groups)),
         ],
-        compiler_params=pltpu.CompilerParams(collective_id=0, has_side_effects=True),
+        compiler_params=pltpu.CompilerParams(collective_id=0, has_side_effects=True, vmem_limit_bytes=28 * 2**20),
     )(stack)
 
 

time: 26.3 us -> 22.9 us (0.87)
  Pallas kernels: 23.3 us -> 19.7 us
  local copies, waits for them, and re-layouts: 2.09 us -> 2.45 us
    pallas_call x1, Pallas kernels: 23.3 us -> 19.7 us  [shards(): pl.pallas_call(functools.partial(kernel, geom), out_shape=(jax.ShapeDtype...]
    unnamed x4, local copies, waits for them, and re-layouts: 2.09 us -> 2.45 us
where the time goes in v2:
time: 22.9 us; the launch traced here: 22.8 us
  Pallas kernels  19.7 us (86%)
  local copies, waits for them, and re-layouts  2.45 us (11%)
  between operations  0.65 us (3%)
    pallas_call x1, Pallas kernels, shards(): pl.pallas_call(functools.partial(kernel, geom), out_shape=(jax.ShapeDtype...  19.7 us
    unnamed x4, local copies, waits for them, and re-layouts  2.45 us

profile of v2, /device:TPU:25, one launch (start us, length us, event | category | flops | bytes accessed | tf_op | source)
XLA Modules:
  0.0 22.8 jit_solution(11497322252176377763)
XLA Ops:
  0.6 0.0 copy-start
  0.6 1.2 %copy-done = bf16[16,16,2048]{2,1,0:T(8,128)(2,1)S(1)} copy-done((bf16[16,16,2048]{2,1,0:T(8,128)(2,1)S(1)}, bf16[16,16,2048]{2,1,0:T(8,128)(2,1)}, u32[]{:S(2)}) %copy-start) | copy-done | bytes 1048600
  1.9 19.7 %shard_map.30 = (f32[16,1024]{1,0:T(8,128)S(1)}, f32[8,512]{1,0:T(8,128)S(1)}) custom-call(bf16[16,16,2048]{2,1,0:T(8,128)(2,1)S(1)} %copy-done), custom_call_target="tpu_custom_call" | custom-call | tf_op jit(solution)/shard_map/pallas_call | solution.py:314
  21.5 0.6 %copy.5 = f32[16,1024]{1,0:T(8,128)} copy(f32[16,1024]{1,0:T(8,128)S(1)} %get-tuple-element.4) | data formatting | bytes 131072
  22.2 0.6 %copy.6 = f32[8,512]{1,0:T(8,128)} copy(f32[8,512]{1,0:T(8,128)S(1)} %get-tuple-element.5) | data formatting | bytes 32768
Async XLA Ops:
  0.6 1.2 %copy-start = (bf16[16,16,2048]{2,1,0:T(8,128)(2,1)S(1)}, bf16[16,16,2048]{2,1,0:T(8,128)(2,1)}, u32[]{:S(2)}) copy-start(bf16[16,16,2048]{2,1,0:T(8,128)(2,1)} %x_hbm.1) | copy-start | bytes 3145732

commit v3 on v2

--- a/solution.py
+++ b/solution.py
@@ -10,11 +10,22 @@
 sharpness = 0.016
 LANES = 128
 HALO = 4
+VMEM_GRANT = 67043328 - 15 * 2**16
 MESH = pl.DeviceIdType.MESH
 
 
 def cols(tile, count):
     return pl.ds(pl.multiple_of(tile * LANES, LANES), count * LANES)
+
+
+def each(start, count, body, width=2):
+    @pl.loop(0, count // width)
+    def _(turn):
+        for k in range(width):
+            body(start + turn * width + k)
+
+    for k in range(count - count % width, count):
+        body(start + k)
 
 
 def from_left(tiles, step, lane):
@@ -153,13 +164,14 @@
     taps[:, 0:LANES] = centre.astype(taps.dtype)
     taps[:, LANES : 2 * LANES] = beside.astype(taps.dtype)
 
-    @pl.loop(0, tiles)
-    def _(t):
+    def own_taps(t):
         wide = xin[:, :, cols(t, 3)].reshape(planes * rows, 3 * LANES)
         both = jnp.dot(wide, taps[...], preferred_element_type=jnp.float32)
         both = both.reshape(planes, rows, 2 * LANES)
         hs[t, :, 8 : 8 + rows, :] = both[:, :, 0:LANES]
         gs[t, :, 8 : 8 + rows, :] = both[:, :, LANES:]
+
+    each(0, tiles, own_taps)
 
     tall = rows + 8
     lane = lax.broadcasted_iota(jnp.int32, (rows, LANES), 1)
@@ -169,41 +181,60 @@
     row_mask = jnp.where((row_tall >= first) & (row_tall < last), 1.0, 0.0).astype(jnp.float32)
 
     def scores(chunk, e_start, e_count):
-        @pl.loop(e_start, e_start + e_count)
-        def _(t):
-            for ref, base in ((top_in, 4), (bot_in, 8 + rows)):
-                both = jnp.dot(
-                    ref[:, cols(t, 3)], taps[...], preferred_element_type=jnp.float32
-                )
-                plain = ref[:, cols(t + 1, 1)].astype(jnp.float32)
-                for p in range(planes):
-                    part = slice(HALO * p, HALO * p + HALO)
-                    hs[t, p, base : base + HALO, :] = both[part, 0:LANES]
-                    gs[t, p, base : base + HALO, :] = both[part, LANES:]
-                    xs[t, p, base : base + HALO, :] = plain[part, :]
-
-        @pl.loop(0, planes)
-        def _(p):
-            for i in range(e_count):
-                t = e_start + i
-                laplace = (
-                    hs[t, p, 6 : 6 + tall, :]
-                    + (gs[t, p, 5 : 5 + tall, :] + gs[t, p, 7 : 7 + tall, :])
-                    - (xs[t, p, 4 : 4 + tall, :] + xs[t, p, 8 : 8 + tall, :])
-                )
-                es[i, :, :] = laplace * laplace * row_mask
-            for i in range(e_count):
-                column = es[i, 0:rows, :]
-                for k in range(1, 5):
-                    column = column + es[i, k : k + rows, :]
-                vs[p, e_start + i + 1] = column
-            flat = [vs[p, chunk * own_tiles + i] for i in range(own_tiles + 2)]
-            right = from_right(flat, 1, lane)
-            pair = [flat[i] + right[i] for i in range(own_tiles + 1)]
-            left = from_left(pair, 2, lane)
-            right2 = from_right(flat, 2, lane)
-            for i in range(own_tiles):
-                ss[p, i] = (pair[i + 1] + left[i] + right2[i + 1]) * sharpness
+        def halo_taps(turn, width):
+            first_tile = e_start + turn
+            wide = [
+                ref[:, cols(first_tile + k, 3)] for k in range(width) for ref in (top_in, bot_in)
+            ]
+            both = jnp.dot(
+                jnp.concatenate(wide, axis=0), taps[...], preferred_element_type=jnp.float32
+            )
+            for k in range(width):
+                t = first_tile + k
+                for side, (ref, base) in enumerate(((top_in, 4), (bot_in, 8 + rows))):
+                    plain = ref[:, cols(t + 1, 1)].astype(jnp.float32)
+                    for p in range(planes):
+                        part = slice(HALO * p, HALO * p + HALO)
+                        row = (2 * k + side) * edge + HALO * p
+                        hs[t, p, base : base + HALO, :] = both[row : row + HALO, 0:LANES]
+                        gs[t, p, base : base + HALO, :] = both[row : row + HALO, LANES:]
+                        xs[t, p, base : base + HALO, :] = plain[part, :]
+
+        width = 3
+
+        @pl.loop(0, e_count // width)
+        def _(turn):
+            halo_taps(turn * width, width)
+
+        if e_count % width:
+            halo_taps(e_count - e_count % width, e_count % width)
+
+        @pl.loop(0, planes // 2)
+        def _(turn):
+            pair_of = [(2 * turn, 0), (2 * turn + 1, 1)]
+            for p, bank in pair_of:
+                for i in range(e_count):
+                    t = e_start + i
+                    laplace = (
+                        hs[t, p, 6 : 6 + tall, :]
+                        + (gs[t, p, 5 : 5 + tall, :] + gs[t, p, 7 : 7 + tall, :])
+                        - (xs[t, p, 4 : 4 + tall, :] + xs[t, p, 8 : 8 + tall, :])
+                    )
+                    es[bank, i, :, :] = laplace * laplace * row_mask
+            for p, bank in pair_of:
+                for i in range(e_count):
+                    column = es[bank, i, 0:rows, :]
+                    for k in range(1, 5):
+                        column = column + es[bank, i, k : k + rows, :]
+                    vs[p, e_start + i + 1] = column
+            for p, bank in pair_of:
+                flat = [vs[p, chunk * own_tiles + i] for i in range(own_tiles + 2)]
+                right = from_right(flat, 1, lane)
+                pair = [flat[i] + right[i] for i in range(own_tiles + 1)]
+                left = from_left(pair, 2, lane)
+                right2 = from_right(flat, 2, lane)
+                for i in range(own_tiles):
+                    ss[p, i] = (pair[i + 1] + left[i] + right2[i + 1]) * sharpness
 
     def finish(chunk, tile, dst):
         peak = ss[0, tile]
@@ -253,15 +284,13 @@
         scores(chunk, e_start, e_count)
         if step < gz_count - 1:
             for group in range(groups):
-                @pl.loop(group * group_tiles, (group + 1) * group_tiles)
-                def _(tile):
-                    finish(chunk, tile, outbox.at[step, tile])
-
+                each(
+                    group * group_tiles, group_tiles,
+                    lambda tile: finish(chunk, tile, outbox.at[step, tile]),
+                )
                 to_peer(step, group).start()
         else:
-            @pl.loop(0, own_tiles)
-            def _(tile):
-                finish(chunk, tile, own.at[tile])
+            each(0, own_tiles, lambda tile: finish(chunk, tile, own.at[tile]))
 
     for group in range(groups):
         for step in range(gz_count - 1):
@@ -332,7 +361,7 @@
             pltpu.VMEM((tiles, planes, rows + 16, LANES), f32),
             pltpu.VMEM((tiles, planes, rows + 16, LANES), f32),
             pltpu.VMEM((tiles, planes, rows + 16, LANES), f32),
-            pltpu.VMEM((spread, rows + 8, LANES), f32),
+            pltpu.VMEM((2, spread, rows + 8, LANES), f32),
             pltpu.VMEM((planes, tiles + 2, rows, LANES), f32),
             pltpu.VMEM((planes, own_tiles, rows, LANES), f32),
             pltpu.VMEM((own_tiles, 2, rows, LANES), f32),
@@ -345,7 +374,7 @@
             pltpu.SemaphoreType.DMA((gz_count - 1, groups)),
             pltpu.SemaphoreType.DMA((gz_count - 1, groups)),
         ],
-        compiler_params=pltpu.CompilerParams(collective_id=0, has_side_effects=True, vmem_limit_bytes=28 * 2**20),
+        compiler_params=pltpu.CompilerParams(collective_id=0, has_side_effects=True, vmem_limit_bytes=VMEM_GRANT),
     )(stack)
 
 

time: 22.9 us -> 19.4 us (0.85)
  Pallas kernels: 19.7 us -> 16.5 us
  local copies, waits for them, and re-layouts: 2.45 us -> 2.09 us
    pallas_call x1, Pallas kernels: 19.7 us -> 16.5 us  [shards(): pl.pallas_call(functools.partial(kernel, geom), out_shape=(jax.ShapeDtype...]
    unnamed x4, local copies, waits for them, and re-layouts: 2.45 us -> 2.09 us
where the time goes in v3:
time: 19.4 us; the launch traced here: 19.2 us
  Pallas kernels  16.5 us (85%)
  local copies, waits for them, and re-layouts  2.09 us (11%)
  between operations  0.65 us (3%)
    pallas_call x1, Pallas kernels, shards(): pl.pallas_call(functools.partial(kernel, geom), out_shape=(jax.ShapeDtype...  16.5 us
    unnamed x4, local copies, waits for them, and re-layouts  2.09 us

profile of v3, /device:TPU:25, one launch (start us, length us, event | category | flops | bytes accessed | tf_op | source)
XLA Modules:
  0.0 19.2 jit_solution(10696434524040850237)
XLA Ops:
  0.6 16.5 %shard_map.30 = (f32[16,1024]{1,0:T(8,128)}, f32[8,512]{1,0:T(8,128)}) custom-call(bf16[16,16,2048]{2,1,0:T(8,128)(2,1)} %x_hbm.1), custom_call_target="tpu_custom_call" | custom-call | tf_op jit(solution)/shard_map/pallas_call | solution.py:343
  17.1 0.0 copy-start
  17.1 1.5 %copy.5 = f32[16,1024]{1,0:T(8,128)} copy(f32[16,1024]{1,0:T(8,128)} %get-tuple-element.4) | data formatting | bytes 131072
  18.6 0.0 copy-done
  18.6 0.6 %copy.6 = f32[8,512]{1,0:T(8,128)} copy(f32[8,512]{1,0:T(8,128)S(1)} %copy-done) | data formatting | bytes 32768
Async XLA Ops:
  17.1 1.5 %copy-start = (f32[8,512]{1,0:T(8,128)S(1)}, f32[8,512]{1,0:T(8,128)}, u32[]{:S(2)}) copy-start(f32[8,512]{1,0:T(8,128)} %get-tuple-element.5) | copy-start | bytes 49156

commit v4 on v3

--- a/solution.py
+++ b/solution.py
@@ -10,7 +10,7 @@
 sharpness = 0.016
 LANES = 128
 HALO = 4
-VMEM_GRANT = 67043328 - 15 * 2**16
+VMEM_GRANT = 32 * 2**20
 MESH = pl.DeviceIdType.MESH
 
 
@@ -45,20 +45,34 @@
     xin, top_in, bot_in, top_out, bot_out, taps, xs, gs, hs, es, vs, ss, own, outbox, inbox, jt,
     load_sem, halo_send, halo_recv, gz_send, gz_recv,
 ):
-    planes, rows, tiles, gz_count, xy_count, own_tiles, groups = geom
+    planes, rows, tiles, gz_count, xy_count, own_tiles = geom
     gz = lax.axis_index("gz")
     xy = lax.axis_index("xy")
     has_up = xy > 0
     has_down = xy < xy_count - 1
 
     if gz_count == 2:
-        near = own_tiles + 2
-        parts = [
-            (jnp.where(gz == 0, tiles - near, 0), near),
-            (jnp.where(gz == 0, 0, near), tiles - near),
+        piece = own_tiles // 2
+        low_side = gz == 1
+
+        def side(start, count):
+            return jnp.where(low_side, start, tiles - start - count)
+
+        sizes = [(0, piece + 2), (piece + 2, own_tiles - piece), (own_tiles + 2, own_tiles - 2)]
+        parts = [(side(start, size), size) for start, size in sizes]
+        spans = [
+            (0, piece, 0, piece + 1),
+            (piece, own_tiles - piece, piece + 1, own_tiles - piece),
+            (own_tiles, own_tiles, own_tiles + 1, own_tiles - 1),
         ]
+        phases = [(0, side(t, n), n, side(e, m), m) for t, n, e, m in spans]
     else:
         parts = [(0, tiles)]
+        phases = []
+        for step in range(gz_count):
+            chunk = lax.rem(gz + 1 + step, gz_count)
+            begin, count = chunk * own_tiles, own_tiles + 2
+            phases.append((step, begin, own_tiles, jnp.clip(begin - 1, 0, tiles - count), count))
 
     def load(part):
         start, size = parts[part]
@@ -180,7 +194,7 @@
     last = jnp.where(has_down, rows + 4, rows + 2)
     row_mask = jnp.where((row_tall >= first) & (row_tall < last), 1.0, 0.0).astype(jnp.float32)
 
-    def scores(chunk, e_start, e_count):
+    def scores(begin, count, e_start, e_count):
         def halo_taps(turn, width):
             first_tile = e_start + turn
             wide = [
@@ -200,7 +214,7 @@
                         gs[t, p, base : base + HALO, :] = both[row : row + HALO, LANES:]
                         xs[t, p, base : base + HALO, :] = plain[part, :]
 
-        width = 3
+        width = e_count if e_count <= 5 else 4
 
         @pl.loop(0, e_count // width)
         def _(turn):
@@ -228,19 +242,19 @@
                         column = column + es[bank, i, k : k + rows, :]
                     vs[p, e_start + i + 1] = column
             for p, bank in pair_of:
-                flat = [vs[p, chunk * own_tiles + i] for i in range(own_tiles + 2)]
+                flat = [vs[p, begin + i] for i in range(count + 2)]
                 right = from_right(flat, 1, lane)
-                pair = [flat[i] + right[i] for i in range(own_tiles + 1)]
+                pair = [flat[i] + right[i] for i in range(count + 1)]
                 left = from_left(pair, 2, lane)
                 right2 = from_right(flat, 2, lane)
-                for i in range(own_tiles):
+                for i in range(count):
                     ss[p, i] = (pair[i + 1] + left[i] + right2[i + 1]) * sharpness
 
-    def finish(chunk, tile, dst):
+    def finish(begin, tile, dst):
         peak = ss[0, tile]
         for p in range(1, planes):
             peak = jnp.maximum(peak, ss[p, tile])
-        place = chunk * own_tiles + tile
+        place = begin + tile
         total, blend = None, None
         for p in range(planes):
             weight = jnp.exp(ss[p, tile] - peak)
@@ -250,13 +264,14 @@
         dst[0] = peak + jnp.log(total)
         dst[1] = blend / total
 
-    group_tiles = own_tiles // groups
-
-    def to_peer(step, group):
-        part = pl.ds(group * group_tiles, group_tiles)
+    sends = phases[:-1]
+
+    def to_peer(index):
+        step, begin, count, _, _ = sends[index]
+        part = pl.ds(lax.rem(begin, own_tiles), count)
         return pltpu.make_async_remote_copy(
             src_ref=outbox.at[step, part], dst_ref=inbox.at[step, part],
-            send_sem=gz_send.at[step, group], recv_sem=gz_recv.at[step, group],
+            send_sem=gz_send.at[index], recv_sem=gz_recv.at[index],
             device_id={"gz": lax.rem(gz + 1 + step, gz_count)}, device_id_type=MESH,
         )
 
@@ -269,41 +284,28 @@
         def _():
             to_down(part).wait_recv()
 
-    for step in range(gz_count):
-        chunk = lax.rem(gz + 1 + step, gz_count)
-        if step < len(parts):
-            halo_arrived(step)
-        if gz_count == 2:
-            if step == 0:
-                e_start, e_count = jnp.where(gz == 0, tiles - own_tiles - 1, 0), own_tiles + 1
-            else:
-                e_start, e_count = jnp.where(gz == 0, 0, own_tiles + 1), own_tiles - 1
+    for index, (step, begin, count, e_start, e_count) in enumerate(phases):
+        if index < len(parts):
+            halo_arrived(index)
+        scores(begin, count, e_start, e_count)
+        if index < len(sends):
+            inside = lax.rem(begin, own_tiles)
+            each(0, count, lambda tile: finish(begin, tile, outbox.at[step, inside + tile]))
+            to_peer(index).start()
         else:
-            e_count = own_tiles + 2
-            e_start = jnp.clip(chunk * own_tiles - 1, 0, tiles - e_count)
-        scores(chunk, e_start, e_count)
-        if step < gz_count - 1:
-            for group in range(groups):
-                each(
-                    group * group_tiles, group_tiles,
-                    lambda tile: finish(chunk, tile, outbox.at[step, tile]),
-                )
-                to_peer(step, group).start()
-        else:
-            each(0, own_tiles, lambda tile: finish(chunk, tile, own.at[tile]))
-
-    for group in range(groups):
-        for step in range(gz_count - 1):
-            to_peer(step, group).wait()
-        for tile in range(group * group_tiles, (group + 1) * group_tiles):
-            logs = [own[tile, 0]] + [inbox[s, tile, 0] for s in range(gz_count - 1)]
-            means = [own[tile, 1]] + [inbox[s, tile, 1] for s in range(gz_count - 1)]
-            peak = functools.reduce(jnp.maximum, logs)
-            shares = [jnp.exp(value - peak) for value in logs]
-            blend = sum(share * mean for share, mean in zip(shares, means))
-            joined = blend / sum(shares)
-            joined_ref[:, tile * LANES : (tile + 1) * LANES] = joined
-            jt[tile] = joined
+            each(0, count, lambda tile: finish(begin, tile, own.at[tile]))
+
+    for index in range(len(sends)):
+        to_peer(index).wait()
+    for tile in range(own_tiles):
+        logs = [own[tile, 0]] + [inbox[s, tile, 0] for s in range(gz_count - 1)]
+        means = [own[tile, 1]] + [inbox[s, tile, 1] for s in range(gz_count - 1)]
+        peak = functools.reduce(jnp.maximum, logs)
+        shares = [jnp.exp(value - peak) for value in logs]
+        blend = sum(share * mean for share, mean in zip(shares, means))
+        joined = blend / sum(shares)
+        joined_ref[:, tile * LANES : (tile + 1) * LANES] = joined
+        jt[tile] = joined
 
     half = rows // 2
     source = lax.broadcasted_iota(jnp.int32, (2 * LANES, LANES), 0)
@@ -334,12 +336,12 @@
     planes, rows, breadth = stack.shape
     tiles = breadth // LANES
     own_tiles = tiles // gz_count
-    groups = 2
-    geom = (planes, rows, tiles, gz_count, xy_count, own_tiles, groups)
+    geom = (planes, rows, tiles, gz_count, xy_count, own_tiles)
     f32 = jnp.float32
     padded = breadth + 2 * LANES
     spread = own_tiles + 4
-    parts = 2 if gz_count == 2 else 1
+    parts = 3 if gz_count == 2 else 1
+    sends = 2 if gz_count == 2 else gz_count - 1
     return pl.pallas_call(
         functools.partial(kernel, geom),
         out_shape=(
@@ -371,11 +373,11 @@
             pltpu.SemaphoreType.DMA((parts,)),
             pltpu.SemaphoreType.DMA((2, parts)),
             pltpu.SemaphoreType.DMA((2, parts)),
-            pltpu.SemaphoreType.DMA((gz_count - 1, groups)),
-            pltpu.SemaphoreType.DMA((gz_count - 1, groups)),
+            pltpu.SemaphoreType.DMA((sends,)),
+            pltpu.SemaphoreType.DMA((sends,)),
         ],
         compiler_params=pltpu.CompilerParams(collective_id=0, has_side_effects=True, vmem_limit_bytes=VMEM_GRANT),
-    )(stack)
+    )(pltpu.with_memory_space_constraint(stack, pltpu.HBM))
 
 
 def solution(mesh):

time: 19.4 us -> 18.1 us (0.933)
  local copies, waits for them, and re-layouts: 2.09 us -> 1.24 us
  Pallas kernels: 16.5 us -> 16 us
    unnamed x4 -> x2, local copies, waits for them, and re-layouts: 2.09 us -> 1.24 us
    pallas_call x1, Pallas kernels: 16.5 us -> 16 us  [shards(): pl.pallas_call(functools.partial(kernel, geom), out_shape=(jax.ShapeDtype...]
where the time goes in v4:
time: 18.1 us; the launch traced here: 17.9 us
  Pallas kernels  16 us (88%)
  local copies, waits for them, and re-layouts  1.24 us (7%)
  between operations  0.64 us (4%)
    pallas_call x1, Pallas kernels, shards(): pl.pallas_call(functools.partial(kernel, geom), out_shape=(jax.ShapeDtype...  16 us
    unnamed x2, local copies, waits for them, and re-layouts  1.24 us

profile of v4, /device:TPU:25, one launch (start us, length us, event | category | flops | bytes accessed | tf_op | source)
XLA Modules:
  0.0 17.9 jit_solution(5115484129253795886)
XLA Ops:
  0.6 16.0 %shard_map.30 = (f32[16,1024]{1,0:T(8,128)S(1)}, f32[8,512]{1,0:T(8,128)S(1)}) custom-call(bf16[16,16,2048]{2,1,0:T(8,128)(2,1)} %x_hbm.1), custom_call_target="tpu_custom_call" | custom-call | tf_op jit(solution)/shard_map/pallas_call | solution.py:345
  16.7 0.6 %copy.5 = f32[16,1024]{1,0:T(8,128)} copy(f32[16,1024]{1,0:T(8,128)S(1)} %get-tuple-element.4) | data formatting | bytes 131072
  17.3 0.6 %copy.6 = f32[8,512]{1,0:T(8,128)} copy(f32[8,512]{1,0:T(8,128)S(1)} %get-tuple-element.5) | data formatting | bytes 32768

commit v5 on v4

--- a/solution.py
+++ b/solution.py
@@ -332,6 +332,17 @@
             to_down(part).wait_send()
 
 
+def write_out(joined_in, pooled_in, joined_out, pooled_out, sems):
+    copies = [
+        pltpu.make_async_copy(joined_in, joined_out, sems.at[0]),
+        pltpu.make_async_copy(pooled_in, pooled_out, sems.at[1]),
+    ]
+    for copy in copies:
+        copy.start()
+    for copy in copies:
+        copy.wait()
+
+
 def shards(gz_count, xy_count, stack):
     planes, rows, breadth = stack.shape
     tiles = breadth // LANES
@@ -342,7 +353,7 @@
     spread = own_tiles + 4
     parts = 3 if gz_count == 2 else 1
     sends = 2 if gz_count == 2 else gz_count - 1
-    return pl.pallas_call(
+    joined, pooled = pl.pallas_call(
         functools.partial(kernel, geom),
         out_shape=(
             jax.ShapeDtypeStruct((rows, own_tiles * LANES), f32),
@@ -378,6 +389,20 @@
         ],
         compiler_params=pltpu.CompilerParams(collective_id=0, has_side_effects=True, vmem_limit_bytes=VMEM_GRANT),
     )(pltpu.with_memory_space_constraint(stack, pltpu.HBM))
+    return pl.pallas_call(
+        write_out,
+        out_shape=(
+            jax.ShapeDtypeStruct(joined.shape, f32),
+            jax.ShapeDtypeStruct(pooled.shape, f32),
+        ),
+        in_specs=[pl.BlockSpec(memory_space=pltpu.VMEM)] * 2,
+        out_specs=(
+            pl.BlockSpec(memory_space=pltpu.HBM),
+            pl.BlockSpec(memory_space=pltpu.HBM),
+        ),
+        scratch_shapes=[pltpu.SemaphoreType.DMA((2,))],
+        compiler_params=pltpu.CompilerParams(vmem_limit_bytes=2**20),
+    )(joined, pooled)
 
 
 def solution(mesh):

time: 18.1 us -> 17.5 us (0.967)
  local copies, waits for them, and re-layouts: 1.24 us -> 0 us
  Pallas kernels: 16 us -> 16.7 us
    unnamed x2 -> x0, local copies, waits for them, and re-layouts: 1.24 us -> none
    pallas_call x0 -> x1, Pallas kernels: none -> 0.65 us  [shards(): pl.pallas_call(write_out, out_shape=(jax.ShapeDtypeStruct(joined.shape, f...]
where the time goes in v5:
time: 17.5 us; the launch traced here: 17.3 us
  Pallas kernels  16.7 us (95%)
  between operations  0.64 us (4%)
    pallas_call x1, Pallas kernels, shards(): pl.pallas_call(functools.partial(kernel, geom), out_shape=(jax.ShapeDtype...  16 us
    pallas_call x1, Pallas kernels, shards(): pl.pallas_call(write_out, out_shape=(jax.ShapeDtypeStruct(joined.shape, f...  0.65 us

profile of v5, /device:TPU:25, one launch (start us, length us, event | category | flops | bytes accessed | tf_op | source)
XLA Modules:
  0.0 17.3 jit_solution(1982009166604006561)
XLA Ops:
  0.6 16.0 %shard_map.30 = (f32[16,1024]{1,0:T(8,128)S(1)}, f32[8,512]{1,0:T(8,128)S(1)}) custom-call(bf16[16,16,2048]{2,1,0:T(8,128)(2,1)} %x_hbm.1), custom_call_target="tpu_custom_call" | custom-call | tf_op jit(solution)/shard_map/pallas_call | solution.py:356
  16.7 0.7 %shard_map.31 = (f32[16,1024]{1,0:T(8,128)}, f32[8,512]{1,0:T(8,128)}) custom-call(f32[16,1024]{1,0:T(8,128)S(1)} %get-tuple-element.4.joined_in, f32[8,512]{1,0:T(8,128)S(1)} %get-tuple-element.5.pooled_in), custom_call_target="tpu_custom_call" | custom-call | tf_op jit(solution)/shard_map/pallas_call | solution.py:392
